TPU v7x, 512 devices: a whole 4x8x8 slice. The times are simulated.
512 devices in a mesh: lon: 64 (over z, x, y_lo), lat: 8 (over y_hi, core).
Axes of the slice: x: 4, y: 8 (y_hi: 4, y_lo: 2; y = y_hi * 2 + y_lo), z: 8, core: 2. Of those that a mesh axis runs over, the one named last changes fastest.
Arguments:
- inputs: bfloat16 [64, 2048, 256], P('lat', 'lon'), may hold values from -6 to 6
- psi_raw: float32 [4, 64, 3, 257], P(None, 'lat'), may hold values from -6 to 6
- widths: int32 [64], P('lat'), may hold values from 1 to 4, as said below
- w_group: bfloat16 [4, 4, 256], replicated, may hold values from -1.5 to 1.5
- w_mix: bfloat16 [256, 256], replicated, may hold values from -0.375 to 0.375
- grad_out: bfloat16 [64, 2048, 256], P('lat', 'lon'), may hold values from -6 to 6
Outputs:
- outputs: bfloat16 [64, 2048, 256], P('lat', 'lon')
- grad_in: bfloat16 [64, 2048, 256], P('lat', 'lon')
Inputs may be any that keep to these rules, and one draw needn't show every extreme that they name: `widths`: let d be a row's distance to the nearer pole (min(i, 63 - i)). A row's width is at most min(4, max(1, 2 * 4 // (d + 1)) + 1); the row nearest each pole has width 4.
All inputs are finite; a program needn't handle non-finite values.
Results may differ from a plain program's by a relative error of at most 0.011.
Values may be sent and summed in bfloat16 or wider, within the bound.
A program may use at most 192 MiB of HBM per device.

v0:
```python
import functools

import jax
import jax.numpy as jnp
from jax import lax
from jax.experimental import pallas as pl
from jax.experimental.pallas import tpu as pltpu
from jax.sharding import PartitionSpec as P

GROUP = 4
SMAX = 4
LANES = 384
CHUNKS = 4
NEAR = (-1, 1, -2, 2)
FAR = (-3, 3, -4, 4)
SLOT = {-2: 0, -1: 1, 0: 2, 1: 3, 2: 4}
FAR_SLOT = {-4: 0, -3: 1, 3: 2, 4: 3}
MESH = pl.DeviceIdType.MESH
F32 = jnp.float32
BF16 = jnp.bfloat16


def iota(shape, axis):
    return lax.broadcasted_iota(jnp.int32, shape, axis)


def kernel(
    n_lon, n_lat,
    x_hbm, psi_hbm, widths, wg_hbm, wm_hbm, go_hbm,
    out_ref, gin_ref,
    psi, wg, wm, go, xw, gw, xe, ge, ff, fr, tf, tb, te, tbe, wbd, cv, acc,
    local_sem, send_sem, recv_sem,
):
    rows, lon_dev, channels = x_hbm.shape
    kernels, taps = psi_hbm.shape[0], psi_hbm.shape[3]
    centre = SMAX * lon_dev
    per = rows // CHUNKS
    wide = lon_dev * 5
    lon, lat = lax.axis_index("lon"), lax.axis_index("lat")
    north, south = lat == 0, lat == n_lat - 1

    def at_lon(by):
        return lax.rem(lon + (by + n_lon), n_lon)

    barrier = pltpu.get_barrier_semaphore()

    def greet(by, up):
        pl.semaphore_signal(
            barrier, inc=1, device_id={"lon": at_lon(by), "lat": lat + up}, device_id_type=MESH
        )

    for by in NEAR:
        greet(by, 0)

    @pl.when(jnp.logical_not(north))
    def _():
        for by in (0,) + NEAR:
            greet(by, -1)

    @pl.when(jnp.logical_not(south))
    def _():
        for by in (0,) + NEAR:
            greet(by, 1)

    polar = jnp.logical_or(north, south)

    @pl.when(polar)
    def _():
        for by in FAR:
            greet(by, 0)

    own = pl.ds(SLOT[0] * lon_dev, lon_dev)
    locals_ = [
        pltpu.make_async_copy(psi_hbm, psi, local_sem.at[0]),
        pltpu.make_async_copy(wg_hbm, wg, local_sem.at[1]),
        pltpu.make_async_copy(wm_hbm, wm, local_sem.at[2]),
        pltpu.make_async_copy(go_hbm, go, local_sem.at[3]),
        pltpu.make_async_copy(x_hbm, xw.at[pl.ds(1, rows), own, :], local_sem.at[4]),
    ]
    for copy in locals_:
        copy.start()

    locals_[0].wait()
    ff[...] = jnp.zeros_like(ff)
    lane = iota((1, taps), 1)
    for i in range(rows):
        reach = widths[i] * lon_dev
        span = jnp.full((1, taps), 3.0 * (2.0 * reach.astype(F32) + 1.0), F32)
        keep = jnp.where(jnp.abs(lane - centre) <= reach, lax.rsqrt(span), 0.0)
        for k in range(kernels):
            ff[i, k, 0:3, 0:taps] = psi[k, i] * keep

    def near_copy(phase, source, at, buf, index, by, up, row, count, target):
        return pltpu.make_async_remote_copy(
            src_ref=source.at[pl.ds(row, count), at, :],
            dst_ref=buf.at[pl.ds(target, count), pl.ds(SLOT[-by] * lon_dev, lon_dev), :],
            send_sem=send_sem.at[phase, index],
            recv_sem=recv_sem.at[phase, index],
            device_id={"lon": at_lon(by), "lat": lat + up},
            device_id_type=MESH,
        )

    def chunk_copies(phase, source, first, at, buf, c):
        return [
            near_copy(phase, source, at, buf, c * 4 + n, by, 0, first + c * per, per, 1 + c * per)
            for n, by in enumerate(NEAR)
        ]

    def edge_copies(phase, source, first, at, buf, up):
        base = 4 * CHUNKS + (0 if up < 0 else 5)
        row, target = (first, rows + 1) if up < 0 else (first + rows - 1, 0)
        return [
            near_copy(phase, source, at, buf, base + n, by, up, row, 1, target)
            for n, by in enumerate((0,) + NEAR)
        ]

    far_rows = ((0, {3: 5, 4: 3}), (1, {3: 4, 4: 2}))

    def far_copies(phase, source, first, at, buf, pole):
        counts = far_rows[phase][1]
        found = []
        for n, by in enumerate(FAR):
            count = counts[abs(by)]
            row = 0 if pole == 0 else rows - count
            found.append(
                pltpu.make_async_remote_copy(
                    src_ref=source.at[pl.ds(first + row, count), at, :],
                    dst_ref=buf.at[
                        pl.ds(1 + row, count), pl.ds(FAR_SLOT[-by] * lon_dev, lon_dev), :
                    ],
                    send_sem=send_sem.at[phase, 4 * CHUNKS + 10 + n],
                    recv_sem=recv_sem.at[phase, 4 * CHUNKS + 10 + n],
                    device_id={"lon": at_lon(by), "lat": lat},
                    device_id_type=MESH,
                )
            )
        return found

    every = pl.ds(0, lon_dev)
    forward = (0, x_hbm, 0, every, xw)
    backward = (1, gw, 1, own, gw)
    forward_far = (0, x_hbm, 0, every, xe)
    backward_far = (1, gw, 1, own, ge)
    inner = (jnp.logical_not(north), jnp.logical_not(south))

    def run(copies, what):
        for copy in copies:
            getattr(copy, what)()

    def edges(phase_args, up, what):
        ok = inner[0] if up < 0 else inner[1]
        if what == "wait_recv":
            ok = inner[1] if up < 0 else inner[0]

        @pl.when(ok)
        def _():
            run(edge_copies(*phase_args, up), what)

    def fars(far_args, pole, what):
        @pl.when(north if pole == 0 else south)
        def _():
            run(far_copies(*far_args, pole), what)

    expected = (
        4
        + 5 * inner[0].astype(jnp.int32)
        + 5 * inner[1].astype(jnp.int32)
        + 4 * polar.astype(jnp.int32)
    )
    pl.semaphore_wait(barrier, expected)

    edges(forward, 1, "start")
    run(chunk_copies(*forward, 0), "start")
    edges(forward, -1, "start")
    for pole in (0, 1):
        fars(forward_far, pole, "start")
    for c in range(1, CHUNKS):
        run(chunk_copies(*forward, c), "start")

    flip = jnp.where(
        iota((LANES, LANES), 0) + iota((LANES, LANES), 1) == 2 * centre, 1.0, 0.0
    ).astype(BF16)
    flipped = jnp.dot(
        ff[...].reshape(rows * kernels * 8, LANES).astype(BF16), flip, preferred_element_type=F32
    )
    fr[pl.ds(1, rows)] = flipped.reshape(rows, kernels, 8, LANES)

    def filter_copy(up):
        n = 4 * CHUNKS + 14 + (0 if up < 0 else 1)
        row, target = (1, rows + 1) if up < 0 else (rows, 0)
        return pltpu.make_async_remote_copy(
            src_ref=fr.at[row],
            dst_ref=fr.at[target],
            send_sem=send_sem.at[0, n],
            recv_sem=recv_sem.at[0, n],
            device_id={"lon": lon, "lat": lat + up},
            device_id_type=MESH,
        )

    @pl.when(inner[0])
    def _():
        filter_copy(-1).start()

    @pl.when(inner[1])
    def _():
        filter_copy(1).start()

    blank = jnp.zeros((wide, channels), BF16)

    @pl.when(north)
    def _():
        xw[0] = blank
        gw[0] = blank
        fr[0] = jnp.zeros(fr.shape[1:], F32)

    @pl.when(south)
    def _():
        xw[rows + 1] = blank
        gw[rows + 1] = blank
        fr[rows + 1] = jnp.zeros(fr.shape[1:], F32)

    def near_block(filters, row, t, k):
        base = jnp.broadcast_to(filters[row, k, t : t + 1, 0:256], (lon_dev, 256))
        return pltpu.roll(base, 256 - 2 * lon_dev, 1, stride=1, stride_axis=0).astype(BF16)

    def far_block(filters, row, t, k):
        lane = iota((lon_dev, 128), 1)

        def part(first):
            return jnp.broadcast_to(
                filters[row, k, t : t + 1, first : first + 128], (lon_dev, 128)
            )

        low = jnp.where(lane < 2 * lon_dev, part(0), 0.0)
        high = jnp.where(lane > 2 * lon_dev, part(128), part(256))
        low = pltpu.roll(low, 0, 1, stride=1, stride_axis=0)
        high = pltpu.roll(high, 128 - lon_dev, 1, stride=1, stride_axis=0)
        return jnp.where(lane < 2 * lon_dev, low, high).astype(BF16)

    def put(dst, index, k, block):
        dst[index, pl.ds(k * lon_dev, lon_dev), :] = block

    @pl.loop(0, rows)
    def _(i):
        for t in range(3):
            for k in range(kernels):
                put(tf, i * 3 + t, k, near_block(ff, i, t, k))

    locals_[1].wait()
    inside = (iota((channels, channels), 0) // GROUP) == (iota((channels, channels), 1) // GROUP)
    for k in range(kernels):
        four = wg[k].astype(F32)
        eight = jnp.concatenate([four, four], axis=0)
        full = jnp.broadcast_to(eight[None], (channels // 8, 8, channels))
        full = full.reshape(channels, channels)
        wbd[pl.ds(k * channels, channels), :] = jnp.where(inside, full, 0.0).astype(BF16)

    for pole in (0, 1):

        @pl.when(north if pole == 0 else south)
        def _():
            for a in range(4):
                row = a if pole == 0 else rows - 1 - a
                for t in range(3):
                    for k in range(kernels):
                        put(te, a * 3 + t, k, far_block(ff, row, t, k))
                        put(tbe, a * 3 + t, k, far_block(fr, row + 1, t, k))

    @pl.when(inner[1])
    def _():
        filter_copy(-1).wait_recv()

    @pl.when(inner[0])
    def _():
        filter_copy(1).wait_recv()

    @pl.loop(0, rows)
    def _(i):
        for t in range(3):
            for k in range(kernels):
                put(tb, i * 3 + t, k, near_block(fr, i + 2 - t, t, k))

    for copy in locals_[2:]:
        copy.wait()

    def far_terms(table, index, buf, row, zero_far):
        if zero_far:
            return jnp.dot(
                table[index, :, lon_dev : 3 * lon_dev],
                buf[row, lon_dev : 3 * lon_dev, :],
                preferred_element_type=F32,
            )
        return jnp.dot(table[index], buf[row], preferred_element_type=F32)

    def conv(table, buf, row_of, c):
        for n in range(per):
            i = c * per + n
            total = None
            for t in range(3):
                term = jnp.dot(
                    table[i * 3 + t, :, 0:wide], buf[row_of(i, t)], preferred_element_type=F32
                )
                total = term if total is None else total + term
            acc[n] = total

    def mix_in(c):
        for n in range(per):
            for k in range(kernels):
                cv[pl.ds(n * lon_dev, lon_dev), pl.ds(k * channels, channels)] = acc[
                    n, pl.ds(k * lon_dev, lon_dev), :
                ].astype(BF16)

    root = 0.7978845608028654
    cubic = 0.044715

    arrived = set()

    def need(phase_args, chunks):
        for c in chunks:
            key = (phase_args[0], c)
            if 0 <= c < CHUNKS and key not in arrived:
                arrived.add(key)
                run(chunk_copies(*phase_args, c), "wait_recv")
            if c == -1:
                edges(phase_args, 1, "wait_recv")
            if c == CHUNKS:
                edges(phase_args, -1, "wait_recv")

    for c in range(CHUNKS):
        need(forward, (c - 1, c, c + 1))
        conv(tf, xw, lambda i, t: i + t, c)
        for pole in (0, 1):
            found = []
            for n in range(per):
                i = c * per + n
                a = i if pole == 0 else rows - 1 - i
                for t in range(3):
                    source = i + t - 1
                    far = source if pole == 0 else rows - 1 - source
                    if a < 4 and far >= 0:
                        found.append((n, a, t, source))
            if not found:
                continue

            @pl.when(north if pole == 0 else south)
            def _():
                if c == (0 if pole == 0 else CHUNKS // 2):
                    run(far_copies(*forward_far, pole), "wait_recv")
                for n, a, t, source in found:
                    acc[n] += far_terms(te, a * 3 + t, xe, source + 1, a >= 2)

        mix_in(c)
        mixed = jnp.dot(cv[...], wbd[...], preferred_element_type=F32).astype(BF16)
        v = jnp.dot(mixed, wm[...], preferred_element_type=F32)
        square = v * v
        th = jnp.tanh(root * v * (1.0 + cubic * square))
        half = 0.5 * (1.0 + th)
        mine = pl.ds(c * per, per)
        shape = (per, lon_dev, channels)
        out_ref[mine] = (v * half).astype(BF16).reshape(shape)
        slope = half + 0.5 * v * (1.0 - th * th) * (root * (1.0 + 3.0 * cubic * square))
        pulled = go[mine].astype(F32).reshape(per * lon_dev, channels) * slope
        back = lax.dot_general(
            pulled.astype(BF16), wm[...], (((1,), (1,)), ((), ())), preferred_element_type=F32
        )
        gw[pl.ds(1 + c * per, per), own, :] = back.astype(BF16).reshape(shape)
        run(chunk_copies(*backward, c), "start")
        if c == 0:
            edges(backward, -1, "start")
        if c == CHUNKS // 2 - 1:
            fars(backward_far, 0, "start")
        if c == CHUNKS - 1:
            edges(backward, 1, "start")
            fars(backward_far, 1, "start")

    for c in (1, 2, 0, 3):
        need(backward, (c - 1, c, c + 1))
        conv(tb, gw, lambda i, t: i + 2 - t, c)
        for pole in (0, 1):
            found = []
            for n in range(per):
                i = c * per + n
                for t in range(3):
                    source = i + 1 - t
                    far = source if pole == 0 else rows - 1 - source
                    if 0 <= far < 4:
                        found.append((n, far, t, source))
            if not found:
                continue

            @pl.when(north if pole == 0 else south)
            def _():
                if c == 1:
                    run(far_copies(*backward_far, pole), "wait_recv")
                for n, a, t, source in found:
                    acc[n] += far_terms(tbe, a * 3 + t, ge, source + 1, a >= 2)

        mix_in(c)
        total = None
        for k in range(kernels):
            at = pl.ds(k * channels, channels)
            term = lax.dot_general(
                cv[:, at], wbd[at, :], (((1,), (1,)), ((), ())), preferred_element_type=F32
            )
            total = term if total is None else total + term
        gin_ref[pl.ds(c * per, per)] = total.astype(BF16).reshape(per, lon_dev, channels)

    for args, far_args in ((forward, forward_far), (backward, backward_far)):
        for c in range(CHUNKS):
            run(chunk_copies(*args, c), "wait_send")
        for up in (-1, 1):
            edges(args, up, "wait_send")
        for pole in (0, 1):
            fars(far_args, pole, "wait_send")

    @pl.when(inner[0])
    def _():
        filter_copy(-1).wait_send()

    @pl.when(inner[1])
    def _():
        filter_copy(1).wait_send()


def body(n_lon, n_lat, inputs, psi_raw, widths, w_group, w_mix, grad_out):
    rows, lon_dev, channels = inputs.shape
    kernels = psi_raw.shape[0]
    wide = 5 * lon_dev
    depth = kernels * lon_dev
    per = rows // CHUNKS
    copies = 4 * CHUNKS + 16
    anywhere = pl.BlockSpec(memory_space=pl.ANY)
    vmem = pl.BlockSpec(memory_space=pltpu.VMEM)
    shape = jax.ShapeDtypeStruct(inputs.shape, BF16)
    return pl.pallas_call(
        functools.partial(kernel, n_lon, n_lat),
        name="disco",
        out_shape=(shape, shape),
        in_specs=[
            anywhere, anywhere, pl.BlockSpec(memory_space=pltpu.SMEM),
            anywhere, anywhere, anywhere,
        ],
        out_specs=(vmem, vmem),
        scratch_shapes=[
            pltpu.VMEM(psi_raw.shape, F32),
            pltpu.VMEM(w_group.shape, BF16),
            pltpu.VMEM(w_mix.shape, BF16),
            pltpu.VMEM(grad_out.shape, BF16),
            pltpu.VMEM((rows + 2, wide, channels), BF16),
            pltpu.VMEM((rows + 2, wide, channels), BF16),
            pltpu.VMEM((rows + 2, 4 * lon_dev, channels), BF16),
            pltpu.VMEM((rows + 2, 4 * lon_dev, channels), BF16),
            pltpu.VMEM((rows, kernels, 8, LANES), F32),
            pltpu.VMEM((rows + 2, kernels, 8, LANES), F32),
            pltpu.VMEM((rows * 3, depth, 256), BF16),
            pltpu.VMEM((rows * 3, depth, 256), BF16),
            pltpu.VMEM((12, depth, 4 * lon_dev), BF16),
            pltpu.VMEM((12, depth, 4 * lon_dev), BF16),
            pltpu.VMEM((kernels * channels, channels), BF16),
            pltpu.VMEM((per * lon_dev, kernels * channels), BF16),
            pltpu.VMEM((per, depth, channels), F32),
            pltpu.SemaphoreType.DMA((5,)),
            pltpu.SemaphoreType.DMA((2, copies)),
            pltpu.SemaphoreType.DMA((2, copies)),
        ],
        compiler_params=pltpu.CompilerParams(
            collective_id=0, has_side_effects=True, vmem_limit_bytes=40 * 1024 * 1024
        ),
        cost_estimate=pl.CostEstimate(
            flops=4_000_000_000, bytes_accessed=2_000_000, transcendentals=65536
        ),
    )(inputs, psi_raw, widths, w_group, w_mix, grad_out)


def solution(mesh):
    return jax.shard_map(
        functools.partial(body, mesh.shape["lon"], mesh.shape["lat"]),
        mesh=mesh,
        in_specs=(
            P("lat", "lon", None),
            P(None, "lat", None, None),
            P("lat"),
            P(),
            P(),
            P("lat", "lon", None),
        ),
        out_specs=(P("lat", "lon", None), P("lat", "lon", None)),
        check_vma=False,
    )
```

profile of v0, /device:TPU:1, one launch (start us, length us, event | category | flops | bytes accessed | tf_op | source)
XLA Modules:
  0.0 45.5 jit_solution(1929607706482367334)
XLA Ops:
  0.6 0.0 copy-start.1
  0.6 0.0 copy-start.3
  0.7 0.0 copy-start.4
  0.7 0.0 copy-start
  0.7 1.0 %copy.8.psi_hbm = f32[4,8,3,257]{3,2,1,0:T(4,128)S(1)} copy(f32[4,8,3,257]{3,1,2,0:T(8,128)} %param.7) | data formatting | bytes 197376 | tf_op args[1]
  1.7 0.0 copy-done.1
  1.7 0.0 copy-done.3
  1.7 0.0 copy-done.4
  1.8 0.0 copy-done
  1.8 0.0 copy-start.2
  1.8 0.9 %copy-done.2 = bf16[8,32,256]{2,1,0:T(8,128)(2,1)S(1)} copy-done((bf16[8,32,256]{2,1,0:T(8,128)(2,1)S(1)}, bf16[8,32,256]{2,1,0:T(8,128)(2,1)}, u32[]{:S(2)}) %copy-start.2) | copy-done | bytes 131096
  2.7 41.5 %disco.1 = (bf16[8,32,256]{2,1,0:T(8,128)(2,1)S(1)}, bf16[8,32,256]{2,1,0:T(8,128)(2,1)S(1)}) custom-call(bf16[8,32,256]{2,1,0:T(8,128)(2,1)S(1)} %copy-done, f32[4,8,3,257]{3,2,1,0:T(4,128)S(1)} %copy.8.psi_hbm, s32[8]{0:T(128)S(1)} %copy-done.4, bf16[4,4,256]{2,1,0:T(4,128)(2,1)S(1)} %copy-done.3, bf16[256,256]{1,0:T(8,128)(2,1)S(1)} %copy-done.1, ...), custom_call_target="tpu_custom_call" | custom-call | flops 4000000000 | bytes 2000000 | tf_op jit(solution)/shard_map/disco/pallas_call | solution.py:435
  44.2 0.7 %copy.11 = bf16[8,32,256]{2,1,0:T(8,128)(2,1)} copy(bf16[8,32,256]{2,1,0:T(8,128)(2,1)S(1)} %get-tuple-element.4) | data formatting | bytes 262144
  44.9 0.7 %copy.12 = bf16[8,32,256]{2,1,0:T(8,128)(2,1)} copy(bf16[8,32,256]{2,1,0:T(8,128)(2,1)S(1)} %get-tuple-element.5) | data formatting | bytes 262144
Async XLA Ops:
  0.6 1.1 %copy-start.1 = (bf16[256,256]{1,0:T(8,128)(2,1)S(1)}, bf16[256,256]{1,0:T(8,128)(2,1)}, u32[]{:S(2)}) copy-start(bf16[256,256]{1,0:T(8,128)(2,1)} %wm_hbm.1) | copy-start | bytes 393220
  0.6 1.1 %copy-start.3 = (bf16[4,4,256]{2,1,0:T(4,128)(2,1)S(1)}, bf16[4,4,256]{2,1,0:T(4,128)(2,1)}, u32[]{:S(2)}) copy-start(bf16[4,4,256]{2,1,0:T(4,128)(2,1)} %wg_hbm.1) | copy-start | bytes 24580
  0.7 1.1 %copy-start.4 = (s32[8]{0:T(128)S(1)}, s32[8]{0:T(128)}, u32[]{:S(2)}) copy-start(s32[8]{0:T(128)} %widths.1) | copy-start | bytes 100
  0.7 1.1 %copy-start = (bf16[8,32,256]{2,1,0:T(8,128)(2,1)S(1)}, bf16[8,32,256]{2,1,0:T(8,128)(2,1)}, u32[]{:S(2)}) copy-start(bf16[8,32,256]{2,1,0:T(8,128)(2,1)} %x_hbm.1) | copy-start | bytes 393220
  1.8 0.9 %copy-start.2 = (bf16[8,32,256]{2,1,0:T(8,128)(2,1)S(1)}, bf16[8,32,256]{2,1,0:T(8,128)(2,1)}, u32[]{:S(2)}) copy-start(bf16[8,32,256]{2,1,0:T(8,128)(2,1)} %go_hbm.1) | copy-start | bytes 393220
where the time goes:
time: 45.7 us; the launch traced here: 45.5 us
  Pallas kernels  41.5 us (91%)
  local copies, waits for them, and re-layouts  3.28 us (7%)
  between operations  0.71 us (2%)
    pallas_call x1, Pallas kernels, body(): pl.pallas_call(functools.partial(kernel, n_lon, n_lat), name='disco', out...  41.5 us
    unnamed x13, local copies, waits for them, and re-layouts  3.28 us

commit v1 on v0

v1 whole, which is shorter than its diff:
```python
import functools

import jax
import jax.numpy as jnp
from jax import lax
from jax.experimental import pallas as pl
from jax.experimental.pallas import tpu as pltpu
from jax.sharding import PartitionSpec as P

GROUP = 4
SMAX = 4
LANES = 384
NEAR = (-1, 1, -2, 2)
FAR = (-3, 3, -4, 4)
SLOT = {-2: 0, -1: 1, 0: 2, 1: 3, 2: 4}
FAR_SLOT = {-4: 0, -3: 1, 3: 2, 4: 3}
MESH = pl.DeviceIdType.MESH
F32 = jnp.float32
BF16 = jnp.bfloat16


def iota(shape, axis):
    return lax.broadcasted_iota(jnp.int32, shape, axis)


def kernel(
    n_lon, n_lat,
    x_hbm, psi_hbm, widths, wg_hbm, wm_hbm, go_hbm,
    out_ref, gin_ref,
    psi, wg, wm, go, xw, gw, xe, ge, ff, fr, fsend, frecv, tf, tb, te, tbe, wbd, cv, acc,
    local_sem, send_sem, recv_sem,
):
    rows, lon_dev, channels = x_hbm.shape
    kernels, taps = psi_hbm.shape[0], psi_hbm.shape[3]
    centre = SMAX * lon_dev
    wide = lon_dev * 5
    lon, lat = lax.axis_index("lon"), lax.axis_index("lat")
    north, south = lat == 0, lat == n_lat - 1
    polar = jnp.logical_or(north, south)
    above, below = jnp.logical_not(north), jnp.logical_not(south)

    def at_lon(by):
        return lax.rem(lon + (by + n_lon), n_lon)

    barrier = pltpu.get_barrier_semaphore()

    def greet(by, up):
        pl.semaphore_signal(
            barrier, inc=1, device_id={"lon": at_lon(by), "lat": lat + up}, device_id_type=MESH
        )

    for by in NEAR:
        greet(by, 0)

    @pl.when(above)
    def _():
        greet(0, -1)

    @pl.when(below)
    def _():
        greet(0, 1)

    @pl.when(polar)
    def _():
        for by in FAR:
            greet(by, 0)

    own = pl.ds(SLOT[0] * lon_dev, lon_dev)
    every = pl.ds(0, lon_dev)
    locals_ = [
        pltpu.make_async_copy(psi_hbm, psi, local_sem.at[0]),
        pltpu.make_async_copy(wg_hbm, wg, local_sem.at[1]),
        pltpu.make_async_copy(wm_hbm, wm, local_sem.at[2]),
        pltpu.make_async_copy(go_hbm, go, local_sem.at[3]),
        pltpu.make_async_copy(x_hbm, xw.at[pl.ds(1, rows), own, :], local_sem.at[4]),
    ]
    for copy in locals_:
        copy.start()

    side = 1 - 2 * lax.rem(lon, 2)

    def slot_at(by):
        return pl.ds(pl.multiple_of((by + 2) * lon_dev, lon_dev), lon_dev)

    def remote(phase, index, src, dst, by, up=0):
        return pltpu.make_async_remote_copy(
            src_ref=src,
            dst_ref=dst,
            send_sem=send_sem.at[phase, index],
            recv_sem=recv_sem.at[phase, index],
            device_id={"lon": at_lon(by), "lat": lat + up},
            device_id_type=MESH,
        )

    def slot(by):
        return pl.ds(SLOT[by] * lon_dev, lon_dev)

    def far_slot(by):
        return pl.ds(FAR_SLOT[by] * lon_dev, lon_dev)

    class Phase:
        def __init__(self, phase, source, first, at, buf, far_buf, groups, far_counts, routes):
            self.phase, self.source, self.first, self.at = phase, source, first, at
            self.buf, self.far_buf, self.groups = buf, far_buf, groups
            self.far_counts, self.routes = far_counts, routes

        def rows_of(self, row, count):
            return self.source.at[pl.ds(self.first + row, count), self.at, :]

        def part(self, g, n, by, at):
            row, count = self.groups[g]
            return remote(
                self.phase, g * 4 + n, self.rows_of(row, count),
                self.buf.at[pl.ds(1 + row, count), at, :], by,
            )

        def group(self, g):
            found = [
                self.part(g, 0, side, slot_at(-side)),
                self.part(g, 2, -2 * side, slot_at(2 * side)),
                self.part(g, 3, 2 * side, slot_at(-2 * side)),
            ]
            if self.routes[g] is None:
                found.append(self.part(g, 1, -side, slot_at(side)))
            return found

        def relay(self, g):
            row, count = self.groups[g]
            rows_ = pl.ds(1 + row, count)
            if self.routes[g] == "plane":
                source, target, by = side, -side, 2 * side
            else:
                source, target, by = 2 * side, side, side
            return [
                remote(
                    self.phase, g * 4 + 1, self.buf.at[rows_, slot_at(source), :],
                    self.buf.at[rows_, slot_at(target), :], by,
                )
            ]

        def landed(self, g, which):
            ats = {0: side, 1: -side, 2: 2 * side, 3: -2 * side}
            return [self.part(g, n, side, slot_at(ats[n])) for n in which]

        def pass_on(self, g):
            if self.routes[g]:
                run(self.landed(g, (0,) if self.routes[g] == "plane" else (2,)), "wait_recv")
                run(self.relay(g), "start")

        def arrive(self, g):
            left = {None: (0, 1, 2, 3), "plane": (1, 2, 3), "pair": (0, 1, 3)}
            run(self.landed(g, left[self.routes[g]]), "wait_recv")

        def sent(self, g):
            run(self.group(g), "wait_send")
            if self.routes[g]:
                run(self.relay(g), "wait_send")

        def lift(self, up):
            row, target = (0, rows + 1) if up < 0 else (rows - 1, 0)
            return [
                remote(
                    self.phase, 12 + (0 if up < 0 else 1), self.rows_of(row, 1),
                    self.buf.at[pl.ds(target, 1), own, :], 0, up,
                )
            ]

        def spread(self, up):
            target = rows + 1 if up < 0 else 0
            return [
                remote(
                    self.phase, 14 + n + (0 if up < 0 else 4),
                    self.buf.at[pl.ds(target, 1), own, :],
                    self.buf.at[pl.ds(target, 1), slot(-by), :], by,
                )
                for n, by in enumerate(NEAR)
            ]

        def far(self, pole, reach):
            count = self.far_counts[reach]
            row = 0 if pole == 0 else rows - count
            return [
                remote(
                    self.phase, 22 + FAR.index(by), self.rows_of(row, count),
                    self.far_buf.at[pl.ds(1 + row, count), far_slot(-by), :], by,
                )
                for by in (-reach, reach)
            ]

        def lifts(self, what):
            for up in (-1, 1):
                ok = (above if up < 0 else below) if what != "wait_recv" else (
                    below if up < 0 else above
                )

                @pl.when(ok)
                def _():
                    run(self.lift(up), what)

        def spreads(self, up, what):
            @pl.when(below if up < 0 else above)
            def _():
                run(self.spread(up), what)

        def fars(self, pole, reach, what):
            @pl.when(north if pole == 0 else south)
            def _():
                run(self.far(pole, reach), what)

    def run(copies, what):
        for copy in copies:
            getattr(copy, what)()

    forward = Phase(0, x_hbm, 0, every, xw, xe, ((0, 3), (5, 3), (3, 2)), {3: 5, 4: 3}, ('plane', 'pair', 'plane'))
    backward = Phase(1, gw, 1, own, gw, ge, ((0, 2), (6, 2), (2, 4)), {3: 4, 4: 2}, ('plane', 'pair', None))

    pl.semaphore_wait(
        barrier,
        4 + above.astype(jnp.int32) + below.astype(jnp.int32) + 4 * polar.astype(jnp.int32),
    )
    forward.lifts("start")
    run(forward.group(0), "start")
    run(forward.group(1), "start")
    for pole in (0, 1):
        for reach in (4, 3):
            forward.fars(pole, reach, "start")

    locals_[0].wait()
    line = iota((rows, LANES), 0)
    reach = jnp.zeros((rows, LANES), jnp.int32)
    for i in range(rows):
        reach = jnp.where(line == i, widths[i] * lon_dev, reach)
    keep = jnp.where(
        jnp.abs(iota((rows, LANES), 1) - centre) <= reach,
        lax.rsqrt(3.0 * (2.0 * reach.astype(F32) + 1.0)),
        0.0,
    )
    ff[:, :, :, 256:LANES] = jnp.zeros((kernels, 3, rows, LANES - 256), F32)
    for k in range(kernels):
        for t in range(3):
            ff[k, t, :, 0:taps] = psi[k, t] * keep[:, 0:taps]

    run(forward.group(2), "start")
    forward.lifts("wait_recv")
    for up in (-1, 1):
        forward.spreads(up, "start")
    for g in range(3):
        forward.pass_on(g)

    flip = jnp.where(
        iota((LANES, LANES), 0) + iota((LANES, LANES), 1) == 2 * centre, 1.0, 0.0
    ).astype(BF16)
    flipped = jnp.dot(
        ff[...].reshape(3 * kernels * rows, LANES).astype(BF16), flip, preferred_element_type=F32
    )
    fr[...] = flipped.reshape(kernels, 3, rows, LANES)
    for k in range(kernels):
        fsend[0, k : k + 1, :] = fr[k, 0, 0:1, :]
        fsend[1, k : k + 1, :] = fr[k, 2, rows - 1 : rows, :]

    def filter_copy(up):
        n = 0 if up < 0 else 1
        return remote(0, 26 + n, fsend.at[n], frecv.at[n], 0, up)

    @pl.when(above)
    def _():
        filter_copy(-1).start()

    @pl.when(below)
    def _():
        filter_copy(1).start()

    blank = jnp.zeros((wide, channels), BF16)

    @pl.when(north)
    def _():
        xw[0] = blank
        gw[0] = blank
        frecv[1] = jnp.zeros(frecv.shape[1:], F32)

    @pl.when(south)
    def _():
        xw[rows + 1] = blank
        gw[rows + 1] = blank
        frecv[0] = jnp.zeros(frecv.shape[1:], F32)

    def near_block(base):
        base = jnp.broadcast_to(base, (lon_dev, 256))
        return pltpu.roll(base, 256 - 2 * lon_dev, 1, stride=1, stride_axis=0).astype(BF16)

    def far_block(filters, row, t, k):
        lane = iota((lon_dev, 128), 1)

        def part(first):
            return jnp.broadcast_to(
                filters[k, t, row : row + 1, first : first + 128], (lon_dev, 128)
            )

        low = jnp.where(lane < 2 * lon_dev, part(0), 0.0)
        high = jnp.where(lane > 2 * lon_dev, part(128), part(256))
        low = pltpu.roll(low, 0, 1, stride=1, stride_axis=0)
        high = pltpu.roll(high, 128 - lon_dev, 1, stride=1, stride_axis=0)
        return jnp.where(lane < 2 * lon_dev, low, high).astype(BF16)

    def put(dst, index, k, block):
        dst[index, pl.ds(k * lon_dev, lon_dev), :] = block

    @pl.loop(0, rows)
    def _(i):
        for t in range(3):
            for k in range(kernels):
                put(tf, i * 3 + t, k, near_block(ff[k, t, pl.ds(i, 1), 0:256]))

    locals_[1].wait()
    inside = (iota((channels, channels), 0) // GROUP) == (iota((channels, channels), 1) // GROUP)
    for k in range(kernels):
        four = wg[k].astype(F32)
        eight = jnp.concatenate([four, four], axis=0)
        full = jnp.broadcast_to(eight[None], (channels // 8, 8, channels))
        full = full.reshape(channels, channels)
        wbd[pl.ds(k * channels, channels), :] = jnp.where(inside, full, 0.0).astype(BF16)

    for pole in (0, 1):

        @pl.when(north if pole == 0 else south)
        def _():
            for a in range(4):
                row = a if pole == 0 else rows - 1 - a
                for t in range(3):
                    for k in range(kernels):
                        put(te, a * 3 + t, k, far_block(ff, row, t, k))
                        put(tbe, a * 3 + t, k, far_block(fr, row, t, k))

    @pl.loop(0, rows)
    def _(source):
        for t in range(3):
            for k in range(kernels):
                put(tb, (source + t) * 3 + t, k, near_block(fr[k, t, pl.ds(source, 1), 0:256]))

    @pl.when(below)
    def _():
        filter_copy(-1).wait_recv()

    @pl.when(above)
    def _():
        filter_copy(1).wait_recv()

    for k in range(kernels):
        put(tb, 3 + 2, k, near_block(frecv[1, k : k + 1, 0:256]))
        put(tb, rows * 3, k, near_block(frecv[0, k : k + 1, 0:256]))

    for copy in locals_[2:]:
        copy.wait()

    def far_term(table, index, buf, row, both):
        if both:
            return jnp.dot(table[index], buf[row], preferred_element_type=F32)
        return jnp.dot(
            table[index, :, lon_dev : 3 * lon_dev],
            buf[row, lon_dev : 3 * lon_dev, :],
            preferred_element_type=F32,
        )

    def conv(table, offset, buf, shift, flipped, span):
        first, count = span
        for n in range(count):
            i = first + n
            total = None
            for t in range(3):
                row = i + (2 - t if flipped else t)
                term = jnp.dot(
                    table[(i + offset) * 3 + t, :, 0:wide], buf[row], preferred_element_type=F32
                )
                total = term if total is None else total + term
            acc[n] = total

    def far_conv(table, buf, flipped, span):
        first, count = span
        for pole in (0, 1):
            found = []
            for n in range(count):
                i = first + n
                for t in range(3):
                    source = i + (1 - t if flipped else t - 1)
                    away = source if pole == 0 else rows - 1 - source
                    a = i if pole == 0 else rows - 1 - i
                    filter_row = away if flipped else a
                    if 0 <= filter_row < 4 and away >= 0:
                        found.append((n, filter_row, t, source))
            if not found:
                continue

            @pl.when(north if pole == 0 else south)
            def _():
                for n, a, t, source in found:
                    acc[n] += far_term(table, a * 3 + t, buf, source + 1, a < 2)

    def gather(span):
        for n in range(span[1]):
            for k in range(kernels):
                cv[pl.ds(n * lon_dev, lon_dev), pl.ds(k * channels, channels)] = acc[
                    n, pl.ds(k * lon_dev, lon_dev), :
                ].astype(BF16)
        return pl.ds(0, span[1] * lon_dev)

    root = 0.7978845608028654
    cubic = 0.044715

    def forward_rows(span):
        first, count = span
        conv(tf, 0, xw, 0, False, span)
        far_conv(te, xe, False, span)
        at = gather(span)
        mixed = jnp.dot(cv[at, :], wbd[...], preferred_element_type=F32).astype(BF16)
        v = jnp.dot(mixed, wm[...], preferred_element_type=F32)
        square = v * v
        th = jnp.tanh(root * v * (1.0 + cubic * square))
        half = 0.5 * (1.0 + th)
        mine = pl.ds(first, count)
        shape = (count, lon_dev, channels)
        slope = half + 0.5 * v * (1.0 - th * th) * (root * (1.0 + 3.0 * cubic * square))
        pulled = go[mine].astype(F32).reshape(count * lon_dev, channels) * slope
        back = lax.dot_general(
            pulled.astype(BF16), wm[...], (((1,), (1,)), ((), ())), preferred_element_type=F32
        )
        gw[pl.ds(1 + first, count), own, :] = back.astype(BF16).reshape(shape)
        out_ref[mine] = (v * half).astype(BF16).reshape(shape)

    def backward_rows(span):
        first, count = span
        conv(tb, 1, gw, 0, True, span)
        far_conv(tbe, ge, True, span)
        at = gather(span)
        total = None
        for k in range(kernels):
            lanes = pl.ds(k * channels, channels)
            term = lax.dot_general(
                cv[at, lanes], wbd[lanes, :], (((1,), (1,)), ((), ())), preferred_element_type=F32
            )
            total = term if total is None else total + term
        gin_ref[pl.ds(first, count)] = total.astype(BF16).reshape(count, lon_dev, channels)

    forward.arrive(0)
    forward.spreads(1, "wait_recv")
    for reach in (4, 3):
        for pole in (0, 1):
            forward.fars(pole, reach, "wait_recv")
    forward_rows((0, 2))
    run(backward.group(0), "start")

    @pl.when(above)
    def _():
        run(backward.lift(-1), "start")

    backward.fars(0, 4, "start")
    forward.arrive(1)
    forward.spreads(-1, "wait_recv")
    forward_rows((6, 2))
    run(backward.group(1), "start")

    @pl.when(below)
    def _():
        run(backward.lift(1), "start")

    backward.fars(1, 4, "start")
    forward.arrive(2)
    forward_rows((2, 4))
    run(backward.group(2), "start")
    for pole in (0, 1):
        backward.fars(pole, 3, "start")
    backward.pass_on(0)
    backward.pass_on(1)
    backward.lifts("wait_recv")
    for up in (-1, 1):
        backward.spreads(up, "start")
    backward.pass_on(2)

    for g in range(3):
        backward.arrive(g)
    for reach in (4, 3):
        for pole in (0, 1):
            backward.fars(pole, reach, "wait_recv")
    backward_rows((2, 4))
    backward.spreads(1, "wait_recv")
    backward_rows((0, 2))
    backward.spreads(-1, "wait_recv")
    backward_rows((6, 2))

    for phase in (forward, backward):
        for g in range(3):
            phase.sent(g)
        phase.lifts("wait_send")
        for up in (-1, 1):
            phase.spreads(up, "wait_send")
        for pole in (0, 1):
            for reach in (4, 3):
                phase.fars(pole, reach, "wait_send")

    @pl.when(above)
    def _():
        filter_copy(-1).wait_send()

    @pl.when(below)
    def _():
        filter_copy(1).wait_send()


def body(n_lon, n_lat, inputs, psi_raw, widths, w_group, w_mix, grad_out):
    rows, lon_dev, channels = inputs.shape
    kernels = psi_raw.shape[0]
    wide = 5 * lon_dev
    depth = kernels * lon_dev
    copies = 28
    psi_raw = jnp.transpose(psi_raw, (0, 2, 1, 3))
    anywhere = pl.BlockSpec(memory_space=pltpu.HBM)
    vmem = pl.BlockSpec(memory_space=pltpu.VMEM)
    shape = jax.ShapeDtypeStruct(inputs.shape, BF16)
    return pl.pallas_call(
        functools.partial(kernel, n_lon, n_lat),
        name="disco",
        out_shape=(pltpu.VMEM(inputs.shape, BF16), pltpu.VMEM(inputs.shape, BF16)),
        in_specs=[
            anywhere, anywhere, pl.BlockSpec(memory_space=pltpu.SMEM),
            anywhere, anywhere, anywhere,
        ],
        out_specs=(vmem, vmem),
        scratch_shapes=[
            pltpu.VMEM(psi_raw.shape, F32),
            pltpu.VMEM(w_group.shape, BF16),
            pltpu.VMEM(w_mix.shape, BF16),
            pltpu.VMEM(grad_out.shape, BF16),
            pltpu.VMEM((rows + 2, wide, channels), BF16),
            pltpu.VMEM((rows + 2, wide, channels), BF16),
            pltpu.VMEM((rows + 2, 4 * lon_dev, channels), BF16),
            pltpu.VMEM((rows + 2, 4 * lon_dev, channels), BF16),
            pltpu.VMEM((kernels, 3, rows, LANES), F32),
            pltpu.VMEM((kernels, 3, rows, LANES), F32),
            pltpu.VMEM((2, 8, LANES), F32),
            pltpu.VMEM((2, 8, LANES), F32),
            pltpu.VMEM((rows * 3, depth, 256), BF16),
            pltpu.VMEM(((rows + 2) * 3, depth, 256), BF16),
            pltpu.VMEM((12, depth, 4 * lon_dev), BF16),
            pltpu.VMEM((12, depth, 4 * lon_dev), BF16),
            pltpu.VMEM((kernels * channels, channels), BF16),
            pltpu.VMEM((4 * lon_dev, kernels * channels), BF16),
            pltpu.VMEM((4, depth, channels), F32),
            pltpu.SemaphoreType.DMA((5,)),
            pltpu.SemaphoreType.DMA((2, copies)),
            pltpu.SemaphoreType.DMA((2, copies)),
        ],
        compiler_params=pltpu.CompilerParams(
            collective_id=0, has_side_effects=True
        ),
        cost_estimate=pl.CostEstimate(
            flops=4_000_000_000, bytes_accessed=2_000_000, transcendentals=65536
        ),
    )(inputs, psi_raw, widths, w_group, w_mix, grad_out)


def solution(mesh):
    return jax.shard_map(
        functools.partial(body, mesh.shape["lon"], mesh.shape["lat"]),
        mesh=mesh,
        in_specs=(
            P("lat", "lon", None),
            P(None, "lat", None, None),
            P("lat"),
            P(),
            P(),
            P("lat", "lon", None),
        ),
        out_specs=(P("lat", "lon", None), P("lat", "lon", None)),
        check_vma=False,
    )
```

time: 45.7 us -> 41.1 us (0.90)
  the two profiles are of different devices: /device:TPU:1 before, /device:TPU:49 now
where the time goes in v1:
time: 41.1 us; the launch traced here: 40.8 us
  Pallas kernels  38.9 us (95%)
  local copies, waits for them, and re-layouts  1.31 us (3%)
  between operations  0.64 us (2%)
    pallas_call x1, Pallas kernels, body(): pl.pallas_call(functools.partial(kernel, n_lon, n_lat), name='disco', out...  38.9 us
    unnamed x2, local copies, waits for them, and re-layouts  1.31 us

profile of v1, /device:TPU:49, one launch (start us, length us, event | category | flops | bytes accessed | tf_op | source)
XLA Modules:
  0.0 40.8 jit_solution(16189703837591170482)
XLA Ops:
  0.6 38.9 %disco.1 = (bf16[8,32,256]{2,1,0:T(8,128)(2,1)S(1)}, bf16[8,32,256]{2,1,0:T(8,128)(2,1)S(1)}) custom-call(bf16[8,32,256]{2,1,0:T(8,128)(2,1)} %x_hbm.1, f32[4,3,8,257]{3,2,1,0:T(8,128)} %bitcast.1, s32[8]{0:T(128)} %widths.1, bf16[4,4,256]{2,1,0:T(4,128)(2,1)} %wg_hbm.1, bf16[256,256]{1,0:T(8,128)(2,1)} %wm_hbm.1, bf16[8,32,256]{2,1,0:T(8,128)(2,1)} %go_hbm.1), custom_call_target="tpu_custom_call" | custom-call | flops 4000000000 | bytes 2000000 | tf_op jit(solution)/shard_map/disco/pallas_call | solution.py:518
  39.5 0.7 %copy.10 = bf16[8,32,256]{2,1,0:T(8,128)(2,1)} copy(bf16[8,32,256]{2,1,0:T(8,128)(2,1)S(1)} %get-tuple-element.2) | data formatting | bytes 262144
  40.2 0.7 %copy.11 = bf16[8,32,256]{2,1,0:T(8,128)(2,1)} copy(bf16[8,32,256]{2,1,0:T(8,128)(2,1)S(1)} %get-tuple-element.3) | data formatting | bytes 262144

commit v2 on v1

--- a/solution.py
+++ b/solution.py
@@ -11,7 +11,6 @@
 SMAX = 4
 LANES = 384
 NEAR = (-1, 1, -2, 2)
-FAR = (-3, 3, -4, 4)
 SLOT = {-2: 0, -1: 1, 0: 2, 1: 3, 2: 4}
 FAR_SLOT = {-4: 0, -3: 1, 3: 2, 4: 3}
 MESH = pl.DeviceIdType.MESH
@@ -36,7 +35,6 @@
     wide = lon_dev * 5
     lon, lat = lax.axis_index("lon"), lax.axis_index("lat")
     north, south = lat == 0, lat == n_lat - 1
-    polar = jnp.logical_or(north, south)
     above, below = jnp.logical_not(north), jnp.logical_not(south)
 
     def at_lon(by):
@@ -60,9 +58,11 @@
     def _():
         greet(0, 1)
 
+    polar = jnp.logical_or(north, south)
+
     @pl.when(polar)
     def _():
-        for by in FAR:
+        for by in (-3, 3):
             greet(by, 0)
 
     own = pl.ds(SLOT[0] * lon_dev, lon_dev)
@@ -99,10 +99,10 @@
         return pl.ds(FAR_SLOT[by] * lon_dev, lon_dev)
 
     class Phase:
-        def __init__(self, phase, source, first, at, buf, far_buf, groups, far_counts, routes):
+        def __init__(self, phase, source, first, at, buf, far_buf, groups, far_count, routes, diagonal):
             self.phase, self.source, self.first, self.at = phase, source, first, at
             self.buf, self.far_buf, self.groups = buf, far_buf, groups
-            self.far_counts, self.routes = far_counts, routes
+            self.far_count, self.routes, self.diagonal = far_count, routes, diagonal
 
         def rows_of(self, row, count):
             return self.source.at[pl.ds(self.first + row, count), self.at, :]
@@ -143,13 +143,12 @@
             return [self.part(g, n, side, slot_at(ats[n])) for n in which]
 
         def pass_on(self, g):
+            run(self.landed(g, (0, 2, 3)), "wait_recv")
             if self.routes[g]:
-                run(self.landed(g, (0,) if self.routes[g] == "plane" else (2,)), "wait_recv")
                 run(self.relay(g), "start")
 
         def arrive(self, g):
-            left = {None: (0, 1, 2, 3), "plane": (1, 2, 3), "pair": (0, 1, 3)}
-            run(self.landed(g, left[self.routes[g]]), "wait_recv")
+            run(self.landed(g, (1,)), "wait_recv")
 
         def sent(self, g):
             run(self.group(g), "wait_send")
@@ -158,15 +157,27 @@
 
         def lift(self, up):
             row, target = (0, rows + 1) if up < 0 else (rows - 1, 0)
-            return [
+            target = pl.ds(target, 1)
+            found = [
                 remote(
                     self.phase, 12 + (0 if up < 0 else 1), self.rows_of(row, 1),
-                    self.buf.at[pl.ds(target, 1), own, :], 0, up,
+                    self.buf.at[target, own, :], 0, up,
                 )
             ]
+            if self.diagonal:
+                found += [
+                    remote(
+                        self.phase, 14 + n + (0 if up < 0 else 4), self.rows_of(row, 1),
+                        self.buf.at[target, slot(-by), :], by, up,
+                    )
+                    for n, by in enumerate(NEAR)
+                ]
+            return found
 
         def spread(self, up):
             target = rows + 1 if up < 0 else 0
+            if self.diagonal:
+                return []
             return [
                 remote(
                     self.phase, 14 + n + (0 if up < 0 else 4),
@@ -176,15 +187,26 @@
                 for n, by in enumerate(NEAR)
             ]
 
-        def far(self, pole, reach):
-            count = self.far_counts[reach]
-            row = 0 if pole == 0 else rows - count
+        def far(self, pole, early):
+            count = self.far_count
+            if early:
+                rows_ = pl.ds(1 if pole == 0 else 1 + rows - count, count)
+                return [
+                    remote(
+                        self.phase, 22 + 2 * (reach - 3) + (s + 1) // 2,
+                        self.buf.at[rows_, slot(2 * s), :],
+                        self.far_buf.at[rows_, far_slot(s * reach), :], -s * (reach - 2),
+                    )
+                    for reach in (3, 4)
+                    for s in (-1, 1)
+                ]
+            row = count if pole == 0 else rows - count - 2
             return [
                 remote(
-                    self.phase, 22 + FAR.index(by), self.rows_of(row, count),
-                    self.far_buf.at[pl.ds(1 + row, count), far_slot(-by), :], by,
+                    self.phase, 28 + (s + 1) // 2, self.rows_of(row, 2),
+                    self.far_buf.at[pl.ds(1 + row, 2), far_slot(-3 * s), :], 3 * s,
                 )
-                for by in (-reach, reach)
+                for s in (-1, 1)
             ]
 
         def lifts(self, what):
@@ -202,28 +224,28 @@
             def _():
                 run(self.spread(up), what)
 
-        def fars(self, pole, reach, what):
+        def fars(self, pole, early, what):
             @pl.when(north if pole == 0 else south)
             def _():
-                run(self.far(pole, reach), what)
+                run(self.far(pole, early), what)
 
     def run(copies, what):
         for copy in copies:
             getattr(copy, what)()
 
-    forward = Phase(0, x_hbm, 0, every, xw, xe, ((0, 3), (5, 3), (3, 2)), {3: 5, 4: 3}, ('plane', 'pair', 'plane'))
-    backward = Phase(1, gw, 1, own, gw, ge, ((0, 2), (6, 2), (2, 4)), {3: 4, 4: 2}, ('plane', 'pair', None))
+    forward = Phase(0, x_hbm, 0, every, xw, xe, ((0, 3), (5, 3), (3, 2)), 3, ('plane', 'pair', 'plane'), False)
+    backward = Phase(1, gw, 1, own, gw, ge, ((0, 2), (6, 2), (2, 4)), 2, ('plane', 'pair', None), True)
 
     pl.semaphore_wait(
         barrier,
-        4 + above.astype(jnp.int32) + below.astype(jnp.int32) + 4 * polar.astype(jnp.int32),
+        4 + above.astype(jnp.int32) + below.astype(jnp.int32) + 2 * polar.astype(jnp.int32),
     )
     forward.lifts("start")
     run(forward.group(0), "start")
     run(forward.group(1), "start")
     for pole in (0, 1):
-        for reach in (4, 3):
-            forward.fars(pole, reach, "start")
+        forward.fars(pole, False, "start")
+    run(forward.group(2), "start")
 
     locals_[0].wait()
     line = iota((rows, LANES), 0)
@@ -240,12 +262,6 @@
         for t in range(3):
             ff[k, t, :, 0:taps] = psi[k, t] * keep[:, 0:taps]
 
-    run(forward.group(2), "start")
-    forward.lifts("wait_recv")
-    for up in (-1, 1):
-        forward.spreads(up, "start")
-    for g in range(3):
-        forward.pass_on(g)
 
     flip = jnp.where(
         iota((LANES, LANES), 0) + iota((LANES, LANES), 1) == 2 * centre, 1.0, 0.0
@@ -311,6 +327,14 @@
             for k in range(kernels):
                 put(tf, i * 3 + t, k, near_block(ff[k, t, pl.ds(i, 1), 0:256]))
 
+    forward.lifts("wait_recv")
+    for up in (-1, 1):
+        forward.spreads(up, "start")
+    forward.pass_on(0)
+    forward.fars(0, True, "start")
+    forward.pass_on(1)
+    forward.fars(1, True, "start")
+
     locals_[1].wait()
     inside = (iota((channels, channels), 0) // GROUP) == (iota((channels, channels), 1) // GROUP)
     for k in range(kernels):
@@ -320,6 +344,13 @@
         full = full.reshape(channels, channels)
         wbd[pl.ds(k * channels, channels), :] = jnp.where(inside, full, 0.0).astype(BF16)
 
+    @pl.loop(0, rows)
+    def _(source):
+        for t in range(3):
+            for k in range(kernels):
+                put(tb, (source + t) * 3 + t, k, near_block(fr[k, t, pl.ds(source, 1), 0:256]))
+
+    forward.pass_on(2)
     for pole in (0, 1):
 
         @pl.when(north if pole == 0 else south)
@@ -330,12 +361,6 @@
                     for k in range(kernels):
                         put(te, a * 3 + t, k, far_block(ff, row, t, k))
                         put(tbe, a * 3 + t, k, far_block(fr, row, t, k))
-
-    @pl.loop(0, rows)
-    def _(source):
-        for t in range(3):
-            for k in range(kernels):
-                put(tb, (source + t) * 3 + t, k, near_block(fr[k, t, pl.ds(source, 1), 0:256]))
 
     @pl.when(below)
     def _():
@@ -442,9 +467,7 @@
 
     forward.arrive(0)
     forward.spreads(1, "wait_recv")
-    for reach in (4, 3):
-        for pole in (0, 1):
-            forward.fars(pole, reach, "wait_recv")
+    forward.fars(0, True, "wait_recv")
     forward_rows((0, 2))
     run(backward.group(0), "start")
 
@@ -452,9 +475,9 @@
     def _():
         run(backward.lift(-1), "start")
 
-    backward.fars(0, 4, "start")
     forward.arrive(1)
     forward.spreads(-1, "wait_recv")
+    forward.fars(1, True, "wait_recv")
     forward_rows((6, 2))
     run(backward.group(1), "start")
 
@@ -462,24 +485,27 @@
     def _():
         run(backward.lift(1), "start")
 
-    backward.fars(1, 4, "start")
     forward.arrive(2)
+    for pole in (0, 1):
+        forward.fars(pole, False, "wait_recv")
     forward_rows((2, 4))
+    for pole in (0, 1):
+        backward.fars(pole, False, "start")
     run(backward.group(2), "start")
-    for pole in (0, 1):
-        backward.fars(pole, 3, "start")
-    backward.pass_on(0)
-    backward.pass_on(1)
     backward.lifts("wait_recv")
     for up in (-1, 1):
         backward.spreads(up, "start")
+    backward.pass_on(0)
+    backward.fars(0, True, "start")
+    backward.pass_on(1)
+    backward.fars(1, True, "start")
     backward.pass_on(2)
 
     for g in range(3):
         backward.arrive(g)
-    for reach in (4, 3):
+    for early in (True, False):
         for pole in (0, 1):
-            backward.fars(pole, reach, "wait_recv")
+            backward.fars(pole, early, "wait_recv")
     backward_rows((2, 4))
     backward.spreads(1, "wait_recv")
     backward_rows((0, 2))
@@ -493,8 +519,8 @@
         for up in (-1, 1):
             phase.spreads(up, "wait_send")
         for pole in (0, 1):
-            for reach in (4, 3):
-                phase.fars(pole, reach, "wait_send")
+            for early in (True, False):
+                phase.fars(pole, early, "wait_send")
 
     @pl.when(above)
     def _():
@@ -510,7 +536,7 @@
     kernels = psi_raw.shape[0]
     wide = 5 * lon_dev
     depth = kernels * lon_dev
-    copies = 28
+    copies = 30
     psi_raw = jnp.transpose(psi_raw, (0, 2, 1, 3))
     anywhere = pl.BlockSpec(memory_space=pltpu.HBM)
     vmem = pl.BlockSpec(memory_space=pltpu.VMEM)

time: 41.1 us -> 42.2 us (1.027)
  the two profiles are of different devices: /device:TPU:49 before, /device:TPU:1 now
where the time goes in v2:
time: 42.2 us; the launch traced here: 42.1 us
  Pallas kernels  40.1 us (95%)
  local copies, waits for them, and re-layouts  1.31 us (3%)
  between operations  0.64 us (2%)
    pallas_call x1, Pallas kernels, body(): pl.pallas_call(functools.partial(kernel, n_lon, n_lat), name='disco', out...  40.1 us
    unnamed x2, local copies, waits for them, and re-layouts  1.31 us

profile of v2, /device:TPU:1, one launch (start us, length us, event | category | flops | bytes accessed | tf_op | source)
XLA Modules:
  0.0 42.1 jit_solution(11428366519927601058)
XLA Ops:
  0.6 40.1 %disco.1 = (bf16[8,32,256]{2,1,0:T(8,128)(2,1)S(1)}, bf16[8,32,256]{2,1,0:T(8,128)(2,1)S(1)}) custom-call(bf16[8,32,256]{2,1,0:T(8,128)(2,1)} %x_hbm.1, f32[4,3,8,257]{3,2,1,0:T(8,128)} %bitcast.1, s32[8]{0:T(128)} %widths.1, bf16[4,4,256]{2,1,0:T(4,128)(2,1)} %wg_hbm.1, bf16[256,256]{1,0:T(8,128)(2,1)} %wm_hbm.1, bf16[8,32,256]{2,1,0:T(8,128)(2,1)} %go_hbm.1), custom_call_target="tpu_custom_call" | custom-call | flops 4000000000 | bytes 2000000 | tf_op jit(solution)/shard_map/disco/pallas_call | solution.py:544
  40.8 0.7 %copy.10 = bf16[8,32,256]{2,1,0:T(8,128)(2,1)} copy(bf16[8,32,256]{2,1,0:T(8,128)(2,1)S(1)} %get-tuple-element.2) | data formatting | bytes 262144
  41.4 0.7 %copy.11 = bf16[8,32,256]{2,1,0:T(8,128)(2,1)} copy(bf16[8,32,256]{2,1,0:T(8,128)(2,1)S(1)} %get-tuple-element.3) | data formatting | bytes 262144

commit v3 on v2

--- a/solution.py
+++ b/solution.py
@@ -25,10 +25,11 @@
 def kernel(
     n_lon, n_lat,
     x_hbm, psi_hbm, widths, wg_hbm, wm_hbm, go_hbm,
-    out_ref, gin_ref,
+    both_ref,
     psi, wg, wm, go, xw, gw, xe, ge, ff, fr, fsend, frecv, tf, tb, te, tbe, wbd, cv, acc,
     local_sem, send_sem, recv_sem,
 ):
+    out_ref, gin_ref = both_ref.at[0], both_ref.at[1]
     rows, lon_dev, channels = x_hbm.shape
     kernels, taps = psi_hbm.shape[0], psi_hbm.shape[3]
     centre = SMAX * lon_dev
@@ -99,16 +100,20 @@
         return pl.ds(FAR_SLOT[by] * lon_dev, lon_dev)
 
     class Phase:
-        def __init__(self, phase, source, first, at, buf, far_buf, groups, far_count, routes, diagonal):
+        def __init__(self, phase, source, first, at, buf, far_buf, groups, far_count, routes):
             self.phase, self.source, self.first, self.at = phase, source, first, at
             self.buf, self.far_buf, self.groups = buf, far_buf, groups
-            self.far_count, self.routes, self.diagonal = far_count, routes, diagonal
+            self.far_count, self.routes = far_count, routes
+
+        def first_of(self, g):
+            row, count = self.groups[g]
+            return jnp.where(south, rows - row - count, row)
 
         def rows_of(self, row, count):
             return self.source.at[pl.ds(self.first + row, count), self.at, :]
 
         def part(self, g, n, by, at):
-            row, count = self.groups[g]
+            row, count = self.first_of(g), self.groups[g][1]
             return remote(
                 self.phase, g * 4 + n, self.rows_of(row, count),
                 self.buf.at[pl.ds(1 + row, count), at, :], by,
@@ -125,8 +130,7 @@
             return found
 
         def relay(self, g):
-            row, count = self.groups[g]
-            rows_ = pl.ds(1 + row, count)
+            rows_ = pl.ds(1 + self.first_of(g), self.groups[g][1])
             if self.routes[g] == "plane":
                 source, target, by = side, -side, 2 * side
             else:
@@ -157,27 +161,15 @@
 
         def lift(self, up):
             row, target = (0, rows + 1) if up < 0 else (rows - 1, 0)
-            target = pl.ds(target, 1)
-            found = [
+            return [
                 remote(
                     self.phase, 12 + (0 if up < 0 else 1), self.rows_of(row, 1),
-                    self.buf.at[target, own, :], 0, up,
+                    self.buf.at[pl.ds(target, 1), own, :], 0, up,
                 )
             ]
-            if self.diagonal:
-                found += [
-                    remote(
-                        self.phase, 14 + n + (0 if up < 0 else 4), self.rows_of(row, 1),
-                        self.buf.at[target, slot(-by), :], by, up,
-                    )
-                    for n, by in enumerate(NEAR)
-                ]
-            return found
 
         def spread(self, up):
             target = rows + 1 if up < 0 else 0
-            if self.diagonal:
-                return []
             return [
                 remote(
                     self.phase, 14 + n + (0 if up < 0 else 4),
@@ -233,8 +225,8 @@
         for copy in copies:
             getattr(copy, what)()
 
-    forward = Phase(0, x_hbm, 0, every, xw, xe, ((0, 3), (5, 3), (3, 2)), 3, ('plane', 'pair', 'plane'), False)
-    backward = Phase(1, gw, 1, own, gw, ge, ((0, 2), (6, 2), (2, 4)), 2, ('plane', 'pair', None), True)
+    forward = Phase(0, x_hbm, 0, every, xw, xe, ((0, 3), (5, 3), (3, 2)), 3, ('pair', 'plane', 'pair'))
+    backward = Phase(1, gw, 1, own, gw, ge, ((0, 2), (6, 2), (2, 4)), 2, ('pair', 'plane', None))
 
     pl.semaphore_wait(
         barrier,
@@ -331,9 +323,9 @@
     for up in (-1, 1):
         forward.spreads(up, "start")
     forward.pass_on(0)
-    forward.fars(0, True, "start")
+    for pole in (0, 1):
+        forward.fars(pole, True, "start")
     forward.pass_on(1)
-    forward.fars(1, True, "start")
 
     locals_[1].wait()
     inside = (iota((channels, channels), 0) // GROUP) == (iota((channels, channels), 1) // GROUP)
@@ -386,10 +378,18 @@
             preferred_element_type=F32,
         )
 
+    def rows_in(span):
+        return [first + n for first, count in span for n in range(count)]
+
+    def scatter(ref, span, shift, at, value):
+        done = 0
+        for first, count in span:
+            piece = value[done * lon_dev : (done + count) * lon_dev]
+            ref[pl.ds(first + shift, count), at, :] = piece.reshape(count, lon_dev, channels)
+            done += count
+
     def conv(table, offset, buf, shift, flipped, span):
-        first, count = span
-        for n in range(count):
-            i = first + n
+        for n, i in enumerate(rows_in(span)):
             total = None
             for t in range(3):
                 row = i + (2 - t if flipped else t)
@@ -400,11 +400,9 @@
             acc[n] = total
 
     def far_conv(table, buf, flipped, span):
-        first, count = span
         for pole in (0, 1):
             found = []
-            for n in range(count):
-                i = first + n
+            for n, i in enumerate(rows_in(span)):
                 for t in range(3):
                     source = i + (1 - t if flipped else t - 1)
                     away = source if pole == 0 else rows - 1 - source
@@ -421,18 +419,18 @@
                     acc[n] += far_term(table, a * 3 + t, buf, source + 1, a < 2)
 
     def gather(span):
-        for n in range(span[1]):
+        count = len(rows_in(span))
+        for n in range(count):
             for k in range(kernels):
                 cv[pl.ds(n * lon_dev, lon_dev), pl.ds(k * channels, channels)] = acc[
                     n, pl.ds(k * lon_dev, lon_dev), :
                 ].astype(BF16)
-        return pl.ds(0, span[1] * lon_dev)
+        return pl.ds(0, count * lon_dev)
 
     root = 0.7978845608028654
     cubic = 0.044715
 
     def forward_rows(span):
-        first, count = span
         conv(tf, 0, xw, 0, False, span)
         far_conv(te, xe, False, span)
         at = gather(span)
@@ -441,18 +439,18 @@
         square = v * v
         th = jnp.tanh(root * v * (1.0 + cubic * square))
         half = 0.5 * (1.0 + th)
-        mine = pl.ds(first, count)
-        shape = (count, lon_dev, channels)
         slope = half + 0.5 * v * (1.0 - th * th) * (root * (1.0 + 3.0 * cubic * square))
-        pulled = go[mine].astype(F32).reshape(count * lon_dev, channels) * slope
+        pull = jnp.concatenate(
+            [go[pl.ds(first, n)].reshape(n * lon_dev, channels) for first, n in span], axis=0
+        )
+        pulled = pull.astype(F32) * slope
         back = lax.dot_general(
             pulled.astype(BF16), wm[...], (((1,), (1,)), ((), ())), preferred_element_type=F32
         )
-        gw[pl.ds(1 + first, count), own, :] = back.astype(BF16).reshape(shape)
-        out_ref[mine] = (v * half).astype(BF16).reshape(shape)
+        scatter(gw, span, 1, own, back.astype(BF16))
+        scatter(out_ref, span, 0, every, (v * half).astype(BF16))
 
     def backward_rows(span):
-        first, count = span
         conv(tb, 1, gw, 0, True, span)
         far_conv(tbe, ge, True, span)
         at = gather(span)
@@ -463,56 +461,9 @@
                 cv[at, lanes], wbd[lanes, :], (((1,), (1,)), ((), ())), preferred_element_type=F32
             )
             total = term if total is None else total + term
-        gin_ref[pl.ds(first, count)] = total.astype(BF16).reshape(count, lon_dev, channels)
-
-    forward.arrive(0)
-    forward.spreads(1, "wait_recv")
-    forward.fars(0, True, "wait_recv")
-    forward_rows((0, 2))
-    run(backward.group(0), "start")
-
-    @pl.when(above)
-    def _():
-        run(backward.lift(-1), "start")
-
-    forward.arrive(1)
-    forward.spreads(-1, "wait_recv")
-    forward.fars(1, True, "wait_recv")
-    forward_rows((6, 2))
-    run(backward.group(1), "start")
-
-    @pl.when(below)
-    def _():
-        run(backward.lift(1), "start")
-
-    forward.arrive(2)
-    for pole in (0, 1):
-        forward.fars(pole, False, "wait_recv")
-    forward_rows((2, 4))
-    for pole in (0, 1):
-        backward.fars(pole, False, "start")
-    run(backward.group(2), "start")
-    backward.lifts("wait_recv")
-    for up in (-1, 1):
-        backward.spreads(up, "start")
-    backward.pass_on(0)
-    backward.fars(0, True, "start")
-    backward.pass_on(1)
-    backward.fars(1, True, "start")
-    backward.pass_on(2)
-
-    for g in range(3):
-        backward.arrive(g)
-    for early in (True, False):
-        for pole in (0, 1):
-            backward.fars(pole, early, "wait_recv")
-    backward_rows((2, 4))
-    backward.spreads(1, "wait_recv")
-    backward_rows((0, 2))
-    backward.spreads(-1, "wait_recv")
-    backward_rows((6, 2))
-
-    for phase in (forward, backward):
+        scatter(gin_ref, span, 0, every, total.astype(BF16))
+
+    def finish(phase):
         for g in range(3):
             phase.sent(g)
         phase.lifts("wait_send")
@@ -522,13 +473,60 @@
             for early in (True, False):
                 phase.fars(pole, early, "wait_send")
 
+    outer, middle = ((0, 2), (6, 2)), ((2, 4),)
+    forward.arrive(0)
+    forward.arrive(1)
+    for up in (1, -1):
+        forward.spreads(up, "wait_recv")
+    for pole in (0, 1):
+        forward.fars(pole, True, "wait_recv")
+    forward_rows(outer)
+
     @pl.when(above)
     def _():
+        run(backward.lift(-1), "start")
+
+    @pl.when(below)
+    def _():
+        run(backward.lift(1), "start")
+
+    run(backward.group(0), "start")
+    run(backward.group(1), "start")
+    forward.arrive(2)
+    for pole in (0, 1):
+        forward.fars(pole, False, "wait_recv")
+    forward_rows(middle)
+    for pole in (0, 1):
+        backward.fars(pole, False, "start")
+    run(backward.group(2), "start")
+    backward.lifts("wait_recv")
+    for up in (-1, 1):
+        backward.spreads(up, "start")
+    backward.pass_on(0)
+    for pole in (0, 1):
+        backward.fars(pole, True, "start")
+    backward.pass_on(1)
+    finish(forward)
+
+    @pl.when(above)
+    def _():
         filter_copy(-1).wait_send()
 
     @pl.when(below)
     def _():
         filter_copy(1).wait_send()
+
+    backward.pass_on(2)
+    for g in range(3):
+        backward.arrive(g)
+    for early in (True, False):
+        for pole in (0, 1):
+            backward.fars(pole, early, "wait_recv")
+    backward_rows(middle)
+    for up in (1, -1):
+        backward.spreads(up, "wait_recv")
+    backward_rows(outer)
+    finish(backward)
 
 
 def body(n_lon, n_lat, inputs, psi_raw, widths, w_group, w_mix, grad_out):
@@ -541,15 +539,15 @@
     anywhere = pl.BlockSpec(memory_space=pltpu.HBM)
     vmem = pl.BlockSpec(memory_space=pltpu.VMEM)
     shape = jax.ShapeDtypeStruct(inputs.shape, BF16)
-    return pl.pallas_call(
+    both = pl.pallas_call(
         functools.partial(kernel, n_lon, n_lat),
         name="disco",
-        out_shape=(pltpu.VMEM(inputs.shape, BF16), pltpu.VMEM(inputs.shape, BF16)),
+        out_shape=pltpu.VMEM((2,) + inputs.shape, BF16),
         in_specs=[
             anywhere, anywhere, pl.BlockSpec(memory_space=pltpu.SMEM),
             anywhere, anywhere, anywhere,
         ],
-        out_specs=(vmem, vmem),
+        out_specs=vmem,
         scratch_shapes=[
             pltpu.VMEM(psi_raw.shape, F32),
             pltpu.VMEM(w_group.shape, BF16),
@@ -581,6 +579,7 @@
             flops=4_000_000_000, bytes_accessed=2_000_000, transcendentals=65536
         ),
     )(inputs, psi_raw, widths, w_group, w_mix, grad_out)
+    return both[0], both[1]
 
 
 def solution(mesh):

time: 42.2 us -> 40 us (0.948)
  the two profiles are of different devices: /device:TPU:1 before, /device:TPU:49 now
where the time goes in v3:
time: 40 us; the launch traced here: 39.8 us
  Pallas kernels  38.5 us (96%)
  local copies, waits for them, and re-layouts  0.72 us (2%)
  between operations  0.64 us (2%)
    pallas_call x1, Pallas kernels, body(): pl.pallas_call(functools.partial(kernel, n_lon, n_lat), name='disco', out...  38.5 us

profile of v3, /device:TPU:49, one launch (start us, length us, event | category | flops | bytes accessed | tf_op | source)
XLA Modules:
  0.0 39.8 jit_solution(8399122011415935189)
XLA Ops:
  0.6 38.5 %disco.1 = bf16[2,8,32,256]{3,2,1,0:T(8,128)(2,1)S(1)} custom-call(bf16[8,32,256]{2,1,0:T(8,128)(2,1)} %x_hbm.1, f32[4,3,8,257]{3,2,1,0:T(8,128)} %bitcast.5, s32[8]{0:T(128)} %widths.1, bf16[4,4,256]{2,1,0:T(4,128)(2,1)} %wg_hbm.1, bf16[256,256]{1,0:T(8,128)(2,1)} %wm_hbm.1, bf16[8,32,256]{2,1,0:T(8,128)(2,1)} %go_hbm.1), custom_call_target="tpu_custom_call" | custom-call | flops 4000000000 | bytes 2000000 | tf_op jit(solution)/shard_map/disco/pallas_call | solution.py:542
  39.1 0.7 %slice_bitcast_fusion = (bf16[8,32,256]{2,1,0:T(8,128)(2,1)}, bf16[8,32,256]{2,1,0:T(8,128)(2,1)}) fusion(bf16[2,8,32,256]{3,2,1,0:T(8,128)(2,1)S(1)} %disco.1), kind=kLoop, calls=%fused_computation | loop fusion | bytes 524288 | tf_op jit(solution)/shard_map/squeeze | solution.py:582

commit v4 on v3

--- a/solution.py
+++ b/solution.py
@@ -226,7 +226,7 @@
             getattr(copy, what)()
 
     forward = Phase(0, x_hbm, 0, every, xw, xe, ((0, 3), (5, 3), (3, 2)), 3, ('pair', 'plane', 'pair'))
-    backward = Phase(1, gw, 1, own, gw, ge, ((0, 2), (6, 2), (2, 4)), 2, ('pair', 'plane', None))
+    backward = Phase(1, gw, 1, own, gw, ge, ((0, 2), (6, 2), (2, 4)), 2, ('plane', 'plane', None))
 
     pl.semaphore_wait(
         barrier,

time: 40 us -> 39.5 us (0.988)
  Pallas kernels: 38.5 us -> 37.8 us
    pallas_call x1, Pallas kernels: 38.5 us -> 37.8 us  [body(): pl.pallas_call(functools.partial(kernel, n_lon, n_lat), name='disco', out...]
where the time goes in v4:
time: 39.5 us; the launch traced here: 39.1 us
  Pallas kernels  37.8 us (96%)
  local copies, waits for them, and re-layouts  0.72 us (2%)
  between operations  0.64 us (2%)
    pallas_call x1, Pallas kernels, body(): pl.pallas_call(functools.partial(kernel, n_lon, n_lat), name='disco', out...  37.8 us

profile of v4, /device:TPU:49, one launch (start us, length us, event | category | flops | bytes accessed | tf_op | source)
XLA Modules:
  0.0 39.1 jit_solution(9947303090517333360)
XLA Ops:
  0.6 37.8 %disco.1 = bf16[2,8,32,256]{3,2,1,0:T(8,128)(2,1)S(1)} custom-call(bf16[8,32,256]{2,1,0:T(8,128)(2,1)} %x_hbm.1, f32[4,3,8,257]{3,2,1,0:T(8,128)} %bitcast.5, s32[8]{0:T(128)} %widths.1, bf16[4,4,256]{2,1,0:T(4,128)(2,1)} %wg_hbm.1, bf16[256,256]{1,0:T(8,128)(2,1)} %wm_hbm.1, bf16[8,32,256]{2,1,0:T(8,128)(2,1)} %go_hbm.1), custom_call_target="tpu_custom_call" | custom-call | flops 4000000000 | bytes 2000000 | tf_op jit(solution)/shard_map/disco/pallas_call | solution.py:542
  38.4 0.7 %slice_bitcast_fusion = (bf16[8,32,256]{2,1,0:T(8,128)(2,1)}, bf16[8,32,256]{2,1,0:T(8,128)(2,1)}) fusion(bf16[2,8,32,256]{3,2,1,0:T(8,128)(2,1)S(1)} %disco.1), kind=kLoop, calls=%fused_computation | loop fusion | bytes 524288 | tf_op jit(solution)/shard_map/squeeze | solution.py:582

commit v5 on v4

--- a/solution.py
+++ b/solution.py
@@ -126,7 +126,7 @@
                 self.part(g, 3, 2 * side, slot_at(-2 * side)),
             ]
             if self.routes[g] is None:
-                found.append(self.part(g, 1, -side, slot_at(side)))
+                found.insert(0, self.part(g, 1, -side, slot_at(side)))
             return found
 
         def relay(self, g):
@@ -235,9 +235,9 @@
     forward.lifts("start")
     run(forward.group(0), "start")
     run(forward.group(1), "start")
+    run(forward.group(2), "start")
     for pole in (0, 1):
         forward.fars(pole, False, "start")
-    run(forward.group(2), "start")
 
     locals_[0].wait()
     line = iota((rows, LANES), 0)

time: 39.5 us -> 39.4 us (level)
  no operation moved by 1% of the time
where the time goes in v5:
time: 39.4 us; the launch traced here: 39.3 us
  Pallas kernels  38 us (96%)
  local copies, waits for them, and re-layouts  0.72 us (2%)
  between operations  0.64 us (2%)
    pallas_call x1, Pallas kernels, body(): pl.pallas_call(functools.partial(kernel, n_lon, n_lat), name='disco', out...  38 us

profile of v5, /device:TPU:49, one launch (start us, length us, event | category | flops | bytes accessed | tf_op | source)
XLA Modules:
  0.0 39.3 jit_solution(8147552749466893903)
XLA Ops:
  0.6 38.0 %disco.1 = bf16[2,8,32,256]{3,2,1,0:T(8,128)(2,1)S(1)} custom-call(bf16[8,32,256]{2,1,0:T(8,128)(2,1)} %x_hbm.1, f32[4,3,8,257]{3,2,1,0:T(8,128)} %bitcast.5, s32[8]{0:T(128)} %widths.1, bf16[4,4,256]{2,1,0:T(4,128)(2,1)} %wg_hbm.1, bf16[256,256]{1,0:T(8,128)(2,1)} %wm_hbm.1, bf16[8,32,256]{2,1,0:T(8,128)(2,1)} %go_hbm.1), custom_call_target="tpu_custom_call" | custom-call | flops 4000000000 | bytes 2000000 | tf_op jit(solution)/shard_map/disco/pallas_call | solution.py:542
  38.6 0.7 %slice_bitcast_fusion = (bf16[8,32,256]{2,1,0:T(8,128)(2,1)}, bf16[8,32,256]{2,1,0:T(8,128)(2,1)}) fusion(bf16[2,8,32,256]{3,2,1,0:T(8,128)(2,1)S(1)} %disco.1), kind=kLoop, calls=%fused_computation | loop fusion | bytes 524288 | tf_op jit(solution)/shard_map/squeeze | solution.py:582

commit v6 on v5

--- a/solution.py
+++ b/solution.py
@@ -235,9 +235,6 @@
     forward.lifts("start")
     run(forward.group(0), "start")
     run(forward.group(1), "start")
-    run(forward.group(2), "start")
-    for pole in (0, 1):
-        forward.fars(pole, False, "start")
 
     locals_[0].wait()
     line = iota((rows, LANES), 0)
@@ -255,6 +252,13 @@
             ff[k, t, :, 0:taps] = psi[k, t] * keep[:, 0:taps]
 
 
+    forward.lifts("wait_recv")
+    for up in (-1, 1):
+        forward.spreads(up, "start")
+    run(forward.group(2), "start")
+    for pole in (0, 1):
+        forward.fars(pole, False, "start")
+
     flip = jnp.where(
         iota((LANES, LANES), 0) + iota((LANES, LANES), 1) == 2 * centre, 1.0, 0.0
     ).astype(BF16)
@@ -319,9 +323,6 @@
             for k in range(kernels):
                 put(tf, i * 3 + t, k, near_block(ff[k, t, pl.ds(i, 1), 0:256]))
 
-    forward.lifts("wait_recv")
-    for up in (-1, 1):
-        forward.spreads(up, "start")
     forward.pass_on(0)
     for pole in (0, 1):
         forward.fars(pole, True, "start")

time: 39.4 us -> 39.4 us (level)
  no operation moved by 1% of the time
where the time goes in v6:
time: 39.4 us; the launch traced here: 39.1 us
  Pallas kernels  37.8 us (96%)
  local copies, waits for them, and re-layouts  0.72 us (2%)
  between operations  0.64 us (2%)
    pallas_call x1, Pallas kernels, body(): pl.pallas_call(functools.partial(kernel, n_lon, n_lat), name='disco', out...  37.8 us

profile of v6, /device:TPU:49, one launch (start us, length us, event | category | flops | bytes accessed | tf_op | source)
XLA Modules:
  0.0 39.1 jit_solution(12282603462511428215)
XLA Ops:
  0.6 37.8 %disco.1 = bf16[2,8,32,256]{3,2,1,0:T(8,128)(2,1)S(1)} custom-call(bf16[8,32,256]{2,1,0:T(8,128)(2,1)} %x_hbm.1, f32[4,3,8,257]{3,2,1,0:T(8,128)} %bitcast.5, s32[8]{0:T(128)} %widths.1, bf16[4,4,256]{2,1,0:T(4,128)(2,1)} %wg_hbm.1, bf16[256,256]{1,0:T(8,128)(2,1)} %wm_hbm.1, bf16[8,32,256]{2,1,0:T(8,128)(2,1)} %go_hbm.1), custom_call_target="tpu_custom_call" | custom-call | flops 4000000000 | bytes 2000000 | tf_op jit(solution)/shard_map/disco/pallas_call | solution.py:543
  38.4 0.7 %slice_bitcast_fusion = (bf16[8,32,256]{2,1,0:T(8,128)(2,1)}, bf16[8,32,256]{2,1,0:T(8,128)(2,1)}) fusion(bf16[2,8,32,256]{3,2,1,0:T(8,128)(2,1)S(1)} %disco.1), kind=kLoop, calls=%fused_computation | loop fusion | bytes 524288 | tf_op jit(solution)/shard_map/squeeze | solution.py:583
